TPU v7x, 256 devices: a whole 4x4x8 slice. The times are simulated.
256 devices in a mesh: dp: 8 (over z_hi, x), space: 32 (over z_lo, y, core).
Axes of the slice: x: 4, y: 4, z: 8 (z_hi: 2, z_lo: 4; z = z_hi * 4 + z_lo), core: 2. Of those that a mesh axis runs over, the one named last changes fastest.
Arguments:
- crop: bfloat16 [8, 4, 128, 64, 64], P('dp', None, 'space'), may hold values from -6 to 6
- filter_one: bfloat16 [3, 3, 3, 4, 32], replicated, may hold values from -0.625 to 0.625
- filter_two: bfloat16 [3, 3, 3, 32, 64], replicated, may hold values from -0.21875 to 0.21875
- cotangent: bfloat16 [8, 64, 32, 16, 16], P('dp', None, 'space'), may hold values from -1 to 1
Outputs:
- features: bfloat16 [8, 64, 32, 16, 16], P('dp', None, 'space')
- grad_one: float32 [3, 3, 3, 4, 32], replicated
- grad_two: float32 [3, 3, 3, 32, 64], replicated
All inputs are finite; a program needn't handle non-finite values.
Results may differ from a plain program's by a relative error of at most 0.0045.
The roundings to bfloat16 on the way count: a program that leaves them out, or rounds other values in their place, can miss the bound.
Values may be sent and summed in bfloat16 or wider, within the bound.
A program may use at most 128 MiB of HBM per device.

v0:
```python
import jax
import jax.numpy as jnp
from jax import lax
from jax.sharding import PartitionSpec as P


def with_halo(shard, sides, width):
    for axis, dim in sides:
        count, length = (lax.axis_size(axis), shard.shape[dim])
        up = [(i, (i + 1) % count) for i in range(count - 1)]
        down = [(j, i) for i, j in up]
        last = lax.slice_in_dim(shard, length - width, length, axis=dim)
        leading = lax.slice_in_dim(shard, 0, width, axis=dim)
        before = lax.ppermute(last, axis, up)
        after = lax.ppermute(leading, axis, down)
        shard = jnp.concatenate([before, shard, after], axis=dim)
    return shard


def leaky(value):
    return jnp.where(value > 0, value, 0.3 * value)


def slope(value):
    return jnp.where(value > 0, 1.0, 0.3)


def pooled(value):
    shape = value.shape
    blocks = value.reshape(shape[0], shape[1], shape[2] // 2, 2, shape[3] // 2, 2, shape[4] // 2, 2)
    return blocks.mean(axis=(3, 5, 7))


def widened(value):
    shape = value.shape
    spread = jnp.broadcast_to(
        value[:, :, :, None, :, None, :, None],
        (shape[0], shape[1], shape[2], 2, shape[3], 2, shape[4], 2),
    )
    return spread.reshape(shape[0], shape[1], 2 * shape[2], 2 * shape[3], 2 * shape[4])


def convolve(source, kernel):
    return lax.conv_general_dilated(
        source,
        kernel,
        (1, 1, 1),
        ((0, 0), (1, 1), (1, 1)),
        dimension_numbers=("NCDHW", "DHWIO", "NCDHW"),
        preferred_element_type=jnp.float32,
    )


def flipped(kernel):
    return jnp.transpose(kernel[::-1, ::-1, ::-1], (0, 1, 2, 4, 3))


def filter_grad(source, gradient):
    planes, extent_y, extent_z = (gradient.shape[2], gradient.shape[3], gradient.shape[4])
    padded = jnp.pad(source, ((0, 0), (0, 0), (0, 0), (1, 1), (1, 1)))
    partials = []
    for offset in range(27):
        shift_a, shift_b, shift_c = (offset // 9, offset // 3 % 3, offset % 3)
        window = padded[
            :,
            :,
            shift_a : shift_a + planes,
            shift_b : shift_b + extent_y,
            shift_c : shift_c + extent_z,
        ]
        partials.append(
            jnp.einsum("bcxyz,bdxyz->cd", window, gradient, preferred_element_type=jnp.float32)
        )
    return jnp.stack(partials).reshape(3, 3, 3, source.shape[1], gradient.shape[1])


def local(crop, filter_one, filter_two, cotangent):
    crop_wide = with_halo(crop, (("space", 2),), 1)
    z_one = convolve(crop_wide, filter_one)
    maps_one = pooled(leaky(z_one)).astype(jnp.bfloat16)
    maps_wide = with_halo(maps_one, (("space", 2),), 1)
    z_two = convolve(maps_wide, filter_two)
    grad_pre_two = (slope(z_two) * widened(cotangent.astype(jnp.float32)) * 0.125).astype(
        jnp.bfloat16
    )
    grad_outer = with_halo(grad_pre_two, (("space", 2),), 1)
    features = pooled(leaky(z_two)).astype(jnp.bfloat16)
    local_two = filter_grad(maps_wide, grad_pre_two)
    back_one = convolve(grad_outer, flipped(filter_two))
    grad_pre_one = (slope(z_one) * widened(back_one) * 0.125).astype(jnp.bfloat16)
    local_one = filter_grad(crop_wide, grad_pre_one)
    grad_one, grad_two = lax.psum((local_one, local_two), ("dp", "space"))
    return (features, grad_one, grad_two)


def solution(mesh):
    placed = (P("dp", None, "space", None, None), P(), P(), P("dp", None, "space", None, None))
    return jax.shard_map(
        local,
        mesh=mesh,
        in_specs=placed,
        out_specs=(P("dp", None, "space", None, None), P(), P()),
        check_vma=False,
    )
```

profile of v0, /device:TPU:1, one launch (start us, length us, event | category | flops | bytes accessed | tf_op | source)
XLA Modules:
  0.0 399.3 jit_solution(16076839817375526808)
XLA Ops:
  7.2 1.2 copy.322
  8.5 4.6 %collective-permute-start = (bf16[1,4,1,64,64]{4,1,3,2,0:T(4,128)(2,1)S(1)}, bf16[1,4,1,64,64]{4,1,3,2,0:T(4,128)(2,1)S(1)}, u32[]{:S(2)}, u32[]{:S(2)}) collective-permute-start(bf16[1,4,1,64,64]{4,1,3,2,0:T(4,128)(2,1)S(1)} %get-tuple-element.20), channel_id=1, source_target_pairs={{0,1},{1,2},{2,3},{3,4},{4,5},{5,6},{6,7},{7,8},{8,9},{9,10},{10,1... | collective-permute-start | bytes 98312 | tf_op jit(solution)/shard_map/ppermute | solution.py:14
  13.1 1.9 collective-permute-start.1
  16.9 1.8 collective-permute-done.1
  19.8 3.7 copy.327
  23.6 1.7 slice.254
  25.2 24.3 %compare_select_fusion = (f32[4,64,8,9,32]{4,2,3,1,0:T(8,128)}, f32[4,64,8,9,32]{4,2,3,1,0:T(8,128)}) fusion(pred[8,9]{0,1:T(8,128)(4,1)S(1)} %copy-done.15, bf16[3,3,3,4,32]{4,3,2,1,0:T(4,128)(2,1)S(1)} %copy-done.14, bf16[4,6,64,1,7,2]{4,0,5,2,1,3:T(4,128)(2,1)S(1)} %slice.254, bf16[4,6,64,1,8,9]{4,0,5,2,1,3:T(4,128)(2,1)} %copy.327), kind=kOutput, calls=%fused_computation.1 | convolution fusion | flops 129835008 | bytes 4989768 | tf_op jit(solution)/shard_map/conv_general_dilated | solution.py:44
  49.5 8.7 %copy.328 = f32[4,64,8,9,32]{1,4,3,2,0:T(8,128)} copy(f32[4,64,8,9,32]{4,2,3,1,0:T(8,128)} %get-tuple-element.10) | data formatting | bytes 4718592 | tf_op jit(solution)/shard_map/jit(_where)/select_n | solution.py:21
  58.2 4.6 %slice_bitcast_fusion.1 = f32[1,32,4,64,64]{3,1,4,2,0:T(8,128)} fusion(f32[4,64,1,72,32]{1,4,3,0,2:T(8,128)} %bitcast.701), kind=kLoop, calls=%fused_computation.14 | loop fusion | bytes 4194304 | tf_op jit(solution)/shard_map/jit(_where)/select_n | solution.py:21
  62.8 9.3 %copy.329 = f32[1,32,4,64,64]{1,4,3,2,0:T(8,128)} copy(f32[1,32,4,64,64]{3,1,4,2,0:T(8,128)} %slice_bitcast_fusion.1) | data formatting | bytes 4194304 | tf_op jit(solution)/shard_map/jit(_where)/select_n | solution.py:21
  72.1 9.1 %reduce_sum.21 = f32[32,2,32,32]{0,3,2,1:T(8,128)S(1)} reduce(f32[32,2,2,32,2,32,2]{0,6,5,4,3,2,1:T(2,128)} %bitcast.698, f32[]{:T(128)} %constant.5.clone.1), dimensions={2,4,6}, to_apply=%region_0.1 | reduce | flops 458752 | bytes 2359300 | tf_op jit(solution)/shard_map/reduce_sum | solution.py:31
  82.5 1.9 collective-permute-start.2
  84.4 2.4 collective-permute-start.3
  88.4 8.7 %copy.335 = f32[4,64,8,9,32]{1,4,3,2,0:T(8,128)} copy(f32[4,64,8,9,32]{4,2,3,1,0:T(8,128)} %get-tuple-element.9) | data formatting | bytes 4718592 | tf_op jit(solution)/shard_map/jit(_where)/select_n | solution.py:25
  97.8 2.3 pad_maximum_fusion
  100.1 3.8 copy.455
  103.9 2.6 pad.12.clone
  106.5 3.0 copy.333
  110.7 4.6 %compare_select_fusion.1 = (f32[2,32,8,5,64]{4,2,3,1,0:T(8,128)S(1)}, f32[2,32,8,5,64]{4,2,3,1,0:T(8,128)}) fusion(bf16[3,3,3,32,64]{4,3,2,1,0:T(8,128)(2,1)S(1)} %copy-done, bf16[32,4,32,1,7,2]{0,4,5,2,1,3:T(8,128)(2,1)S(1)} %slice.258, bf16[32,4,32,1,8,5]{0,4,5,2,1,3:T(8,128)(2,1)} %copy.333, pred[8,5]{0,1:T(8,128)(4,1)S(1)} %copy-done.16), kind=kOutput, calls=%fused_computation.34 | convolution fusion | flops 279412736 | bytes 1863720 | tf_op jit(solution)/shard_map/conv_general_dilated | solution.py:44
  131.9 1.5 fusion.39
  136.9 3.1 collective-permute-start.4
  140.0 2.1 collective-permute-start.5
  142.1 1.6 copy.334
  144.9 2.8 collective-permute-done.5
  148.9 5.1 %fusion.32 = f32[2,32,8,5,32]{4,2,3,1,0:T(8,128)S(1)} fusion(bf16[3,3,3,32,64]{4,3,2,1,0:T(8,128)(2,1)S(1)} %copy-done, bf16[64,4,32,1,7,2]{0,4,5,2,1,3:T(8,128)(2,1)S(1)} %slice.264, bf16[64,4,32,1,8,5]{0,4,5,2,1,3:T(8,128)(2,1)S(1)} %copy.339, pred[8,5]{0,1:T(8,128)(4,1)S(1)} %copy-done.16), kind=kOutput, calls=%fused_computation.36 | convolution fusion | flops 280051712 | bytes 1323048 | tf_op jit(solution)/shard_map/conv_general_dilated | solution.py:44
  155.0 7.6 %broadcast_in_dim.44 = f32[32,2,2,32,2,32,2]{0,6,5,4,3,2,1:T(2,128)} broadcast(f32[32,2,32,32]{0,3,2,1:T(8,128)S(1)} %copy.341), dimensions={0,1,3,5} | broadcast | bytes 2359296 | tf_op jit(solution)/shard_map/broadcast_in_dim | solution.py:36
  162.6 7.8 %copy.342 = f32[1,32,4,64,64]{3,1,4,2,0:T(8,128)} copy(f32[1,32,4,64,64]{1,4,3,2,0:T(8,128)} %bitcast.699) | data formatting | bytes 4194304 | tf_op jit(solution)/shard_map/broadcast_in_dim | solution.py:36
  170.4 5.8 %fusion.14 = bf16[32,4,64,64]{2,0,3,1:T(8,128)(2,1)} fusion(f32[1,32,4,64,64]{3,1,4,2,0:T(8,128)} %copy.342, f32[4,64,1,72,32]{1,4,3,0,2:T(8,128)} %bitcast.700), kind=kLoop, calls=%fused_computation.20 | loop fusion | flops 1572864 | bytes 5242880 | tf_op jit(solution)/shard_map/reshape.3
  176.3 5.7 %copy.343 = bf16[32,4,64,64]{3,0,2,1:T(8,128)(2,1)S(1)} copy(bf16[32,4,64,64]{2,0,3,1:T(8,128)(2,1)} %fusion.14) | data formatting | bytes 2097152 | tf_op jit(solution)/shard_map/reshape.3
  201.1 85.7 %psum.14 = f32[3,3,3,4,32]{4,3,2,1,0:T(4,128)} all-reduce(f32[3,3,3,4,32]{4,3,2,1,0:T(4,128)S(1)} %bitcast.714), channel_id=1, replica_groups=mesh['dp'=8,'space'=32] {'dp','space'}, use_global_device_ids=true, to_apply=%region_3.4 | all-reduce | flops 3456 | bytes 27648 | tf_op jit(solution)/shard_map/psum | solution.py:92
  286.8 103.6 %all-reduce.4.cloned.1.call-done = f32[3,3,3,32,64]{4,3,2,1,0:T(8,128)} async-done(((f32[3,3,3,32,64]{4,3,2,1,0:T(8,128)}), f32[3,3,3,32,64]{4,3,2,1,0:T(8,128)}) %all-reduce.4.cloned.1.call-update) | async-done | bytes 221200 | tf_op jit(solution)/shard_map/psum | solution.py:92
  390.4 1.8 copy.566
  (122 shorter events, 49.9 us)
Async XLA Ops:
  7.2 103.6 %copy-start = (bf16[3,3,3,32,64]{4,3,2,1,0:T(8,128)(2,1)S(1)}, bf16[3,3,3,32,64]{4,3,2,1,0:T(8,128)(2,1)}, u32[]{:S(2)}) copy-start(bf16[3,3,3,32,64]{4,3,2,1,0:T(8,128)(2,1)} %param.6) | copy-start | bytes 331780
  7.2 383.2 %all-reduce.4.cloned.1.call-start = ((), (), s32[]{:S(2)}) async-start(), calls=%async_computation | async-start | bytes 884736 | tf_op jit(solution)/shard_map/psum | solution.py:92
  8.5 6.5 %collective-permute-start = (bf16[1,4,1,64,64]{4,1,3,2,0:T(4,128)(2,1)S(1)}, bf16[1,4,1,64,64]{4,1,3,2,0:T(4,128)(2,1)S(1)}, u32[]{:S(2)}, u32[]{:S(2)}) collective-permute-start(bf16[1,4,1,64,64]{4,1,3,2,0:T(4,128)(2,1)S(1)} %get-tuple-element.20), channel_id=1, source_target_pairs={{0,1},{1,2},{2,3},{3,4},{4,5},{5,6},{6,7},{7,8},{8,9},{9,10},{10,1... | collective-permute-start | bytes 98312 | tf_op jit(solution)/shard_map/ppermute | solution.py:14
  13.1 5.6 %collective-permute-start.1 = (bf16[1,4,1,64,64]{4,1,3,2,0:T(4,128)(2,1)S(1)}, bf16[1,4,1,64,64]{4,1,3,2,0:T(4,128)(2,1)S(1)}, u32[]{:S(2)}, u32[]{:S(2)}) collective-permute-start(bf16[1,4,1,64,64]{4,1,3,2,0:T(4,128)(2,1)S(1)} %get-tuple-element.19), channel_id=1, source_target_pairs={{1,0},{2,1},{3,2},{4,3},{5,4},{6,5},{7,6},{8,7},{9,8},{10,9},{11,1... | collective-permute-start | bytes 98312 | tf_op jit(solution)/shard_map/ppermute | solution.py:15
  15.0 0.6 copy-start.10
  18.7 0.6 copy-start.8
  19.8 5.4 %copy-start.14 = (bf16[3,3,3,4,32]{4,3,2,1,0:T(4,128)(2,1)S(1)}, bf16[3,3,3,4,32]{4,3,2,1,0:T(4,128)(2,1)}, u32[]{:S(2)}) copy-start(bf16[3,3,3,4,32]{4,3,2,1,0:T(4,128)(2,1)} %param.5) | copy-start | bytes 20740
  19.8 5.4 %copy-start.15 = (pred[8,9]{0,1:T(8,128)(4,1)S(1)}, pred[8,9]{0,1:T(8,128)(4,1)}, u32[]{:S(2)}) copy-start(pred[8,9]{0,1:T(8,128)(4,1)} %constant.39) | copy-start | bytes 220
  81.6 5.2 %copy-start.13 = (bf16[1,64,1,16,16]{1,4,3,2,0:T(8,128)(2,1)S(1)}, bf16[1,64,1,16,16]{1,4,3,2,0:T(8,128)(2,1)}, u32[]{:S(2)}) copy-start(bf16[1,64,1,16,16]{1,4,3,2,0:T(8,128)(2,1)} %param.7) | copy-start | bytes 98308
  81.6 5.9 %copy-start.3 = (bf16[1,4,4,64,64]{4,3,2,1,0:T(8,128)(2,1)S(1)}, bf16[1,4,4,64,64]{4,3,2,1,0:T(8,128)(2,1)}, u32[]{:S(2)}) copy-start(bf16[1,4,4,64,64]{4,3,2,1,0:T(8,128)(2,1)} %param.4) | copy-start | bytes 393220
  82.5 14.6 %collective-permute-start.2 = (bf16[1,32,1,32,32]{4,1,3,2,0:T(8,128)(2,1)}, bf16[1,32,1,32,32]{4,1,3,2,0:T(8,128)(2,1)S(1)}, u32[]{:S(2)}, u32[]{:S(2)}) collective-permute-start(bf16[1,32,1,32,32]{4,1,3,2,0:T(8,128)(2,1)} %get-tuple-element.17), channel_id=1, source_target_pairs={{0,1},{1,2},{2,3},{3,4},{4,5},{5,6},{6,7},{7,8},{8,9},{9,10},{10,1... | collective-permute-start | bytes 196616 | tf_op jit(solution)/shard_map/ppermute | solution.py:14
  84.4 13.4 %collective-permute-start.3 = (bf16[1,32,1,32,32]{4,1,3,2,0:T(8,128)(2,1)S(1)}, bf16[1,32,1,32,32]{4,1,3,2,0:T(8,128)(2,1)}, u32[]{:S(2)}, u32[]{:S(2)}) collective-permute-start(bf16[1,32,1,32,32]{4,1,3,2,0:T(8,128)(2,1)S(1)} %get-tuple-element.18), channel_id=1, source_target_pairs={{1,0},{2,1},{3,2},{4,3},{5,4},{6,5},{7,6},{8,7},{9,8},{10,9},{11,1... | collective-permute-start | bytes 196616 | tf_op jit(solution)/shard_map/ppermute | solution.py:15
  97.1 0.7 copy-start.6
  106.5 4.2 %copy-start.16 = (pred[8,5]{0,1:T(8,128)(4,1)S(1)}, pred[8,5]{0,1:T(8,128)(4,1)}, u32[]{:S(2)}) copy-start(pred[8,5]{0,1:T(8,128)(4,1)} %constant.38) | copy-start | bytes 124
  115.4 0.9 copy-start.4
  118.3 1.9 copy-start.7
  134.8 2.0 copy-start.2
  136.0 0.8 copy-start.5
  136.9 8.1 %collective-permute-start.4 = (bf16[1,64,1,32,32]{1,3,4,2,0:T(8,128)(2,1)S(1)}, bf16[1,64,1,32,32]{1,3,4,2,0:T(8,128)(2,1)S(1)}, u32[]{:S(2)}, u32[]{:S(2)}) collective-permute-start(bf16[1,64,1,32,32]{1,3,4,2,0:T(8,128)(2,1)S(1)} %get-tuple-element.15), channel_id=1, source_target_pairs={{0,1},{1,2},{2,3},{3,4},{4,5},{5,6},{6,7},{7,8},{8,9},{9,10},{10,1... | collective-permute-start | bytes 393224 | tf_op jit(solution)/shard_map/ppermute | solution.py:14
  140.0 7.7 %collective-permute-start.5 = (bf16[1,64,1,32,32]{1,3,4,2,0:T(8,128)(2,1)S(1)}, bf16[1,64,1,32,32]{1,3,4,2,0:T(8,128)(2,1)S(1)}, u32[]{:S(2)}, u32[]{:S(2)}) collective-permute-start(bf16[1,64,1,32,32]{1,3,4,2,0:T(8,128)(2,1)S(1)} %get-tuple-element.16), channel_id=1, source_target_pairs={{1,0},{2,1},{3,2},{4,3},{5,4},{6,5},{7,6},{8,7},{9,8},{10,9},{11,1... | collective-permute-start | bytes 393224 | tf_op jit(solution)/shard_map/ppermute | solution.py:15
  183.3 1.5 copy-start.11
  189.6 1.6 copy-start.1
  189.6 1.6 copy-start.12
  196.1 1.5 copy-start.9
Sparse Core Ops, SparseCore 0:
  136.9 253.4 all-reduce.3
where the time goes:
time: 407 us; the launch traced here: 399 us
  waiting for transfers between devices  108 us (27%)
  blocking collectives  85.7 us (21%)
  local copies, waits for them, and re-layouts  83.9 us (21%)
  matrix products  71.1 us (17%)
  other arithmetic  19.3 us (5%)
  starting transfers between devices  16.1 us (4%)
  between operations  14.9 us (4%)
    psum x1, waiting for transfers between devices, local(): grad_one, grad_two = lax.psum((local_one, local_two), ('dp', 'space'))  104 us
    psum x1, blocking collectives, local(): grad_one, grad_two = lax.psum((local_one, local_two), ('dp', 'space'))  85.7 us
    dot_general x54, matrix products, filter_grad(): jnp.einsum('bcxyz,bdxyz->cd', window, gradient, preferred_element_type=jn...  37.1 us
    conv_general_dilated x3, matrix products, convolve(): lax.conv_general_dilated(source, kernel, (1, 1, 1), ((0, 0), (1, 1), (1,...  34 us
    select_n x4, local copies, waits for them, and re-layouts, leaky(): return jnp.where(value > 0, value, 0.3 * value)  24.2 us
    broadcast_in_dim x6, local copies, waits for them, and re-layouts, widened(): jnp.broadcast_to(value[:, :, :, None, :, None, :, None], (shape[0], shape...  17.1 us
    unnamed x41, local copies, waits for them, and re-layouts  12.5 us
    conv_general_dilated x7, local copies, waits for them, and re-layouts, convolve(): lax.conv_general_dilated(source, kernel, (1, 1, 1), ((0, 0), (1, 1), (1,...  10.5 us
  transfers between devices with their start and end apart: 7, of which 3 were waited for; matrix products, arithmetic and copies ran while one was open for 17% of the time, Pallas kernels for 0%

commit v1 on v0

--- a/solution.py
+++ b/solution.py
@@ -89,7 +89,7 @@
     back_one = convolve(grad_outer, flipped(filter_two))
     grad_pre_one = (slope(z_one) * widened(back_one) * 0.125).astype(jnp.bfloat16)
     local_one = filter_grad(crop_wide, grad_pre_one)
-    grad_one, grad_two = lax.psum((local_one, local_two), ("dp", "space"))
+    grad_one, grad_two = lax.psum(lax.psum((local_one, local_two), "space"), "dp")
     return (features, grad_one, grad_two)
 
 

time: 407 us -> 616 us (1.51)
  the two profiles are of different devices: /device:TPU:1 before, /device:TPU:0 now
where the time goes in v1:
time: 616 us; the launch traced here: 609 us
  waiting for transfers between devices  214 us (35%)
  blocking collectives  192 us (31%)
  local copies, waits for them, and re-layouts  83.9 us (14%)
  matrix products  71.1 us (12%)
  other arithmetic  19.3 us (3%)
  between operations  14.9 us (2%)
  starting transfers between devices  13.3 us (2%)
    psum x1, waiting for transfers between devices, local(): lax.psum((local_one, local_two), 'space')  214 us
    psum x1, blocking collectives, local(): lax.psum((local_one, local_two), 'space')  138 us
    psum x1, blocking collectives, local(): lax.psum(lax.psum((local_one, local_two), 'space'), 'dp')  53.9 us
    dot_general x54, matrix products, filter_grad(): jnp.einsum('bcxyz,bdxyz->cd', window, gradient, preferred_element_type=jn...  37.1 us
    conv_general_dilated x3, matrix products, convolve(): lax.conv_general_dilated(source, kernel, (1, 1, 1), ((0, 0), (1, 1), (1,...  34 us
    select_n x4, local copies, waits for them, and re-layouts, leaky(): return jnp.where(value > 0, value, 0.3 * value)  24.2 us
    broadcast_in_dim x6, local copies, waits for them, and re-layouts, widened(): jnp.broadcast_to(value[:, :, :, None, :, None, :, None], (shape[0], shape...  17.1 us
    unnamed x41, local copies, waits for them, and re-layouts  12.5 us
  transfers between devices with their start and end apart: 8, of which 2 were waited for; matrix products, arithmetic and copies ran while one was open for 11% of the time, Pallas kernels for 0%

profile of v1, /device:TPU:0, one launch (start us, length us, event | category | flops | bytes accessed | tf_op | source)
XLA Modules:
  0.0 608.6 jit_solution(12801883025810173174)
XLA Ops:
  7.2 1.2 copy.322
  8.5 1.3 collective-permute-start
  9.8 1.3 collective-permute-start.1
  14.2 3.7 copy.327
  17.9 1.7 slice.254
  19.6 24.2 %compare_select_fusion = (f32[4,64,8,9,32]{4,2,3,1,0:T(8,128)}, f32[4,64,8,9,32]{4,2,3,1,0:T(8,128)}) fusion(pred[8,9]{0,1:T(8,128)(4,1)S(1)} %copy-done.15, bf16[3,3,3,4,32]{4,3,2,1,0:T(4,128)(2,1)S(1)} %copy-done.14, bf16[4,6,64,1,7,2]{4,0,5,2,1,3:T(4,128)(2,1)S(1)} %slice.254, bf16[4,6,64,1,8,9]{4,0,5,2,1,3:T(4,128)(2,1)} %copy.327), kind=kOutput, calls=%fused_computation.1 | convolution fusion | flops 129835008 | bytes 4989768 | tf_op jit(solution)/shard_map/conv_general_dilated | solution.py:44
  43.8 8.7 %copy.328 = f32[4,64,8,9,32]{1,4,3,2,0:T(8,128)} copy(f32[4,64,8,9,32]{4,2,3,1,0:T(8,128)} %get-tuple-element.10) | data formatting | bytes 4718592 | tf_op jit(solution)/shard_map/jit(_where)/select_n | solution.py:21
  52.5 4.6 slice_bitcast_fusion.1
  57.1 9.3 %copy.329 = f32[1,32,4,64,64]{1,4,3,2,0:T(8,128)} copy(f32[1,32,4,64,64]{3,1,4,2,0:T(8,128)} %slice_bitcast_fusion.1) | data formatting | bytes 4194304 | tf_op jit(solution)/shard_map/jit(_where)/select_n | solution.py:21
  66.4 9.1 %reduce_sum.21 = f32[32,2,32,32]{0,3,2,1:T(8,128)S(1)} reduce(f32[32,2,2,32,2,32,2]{0,6,5,4,3,2,1:T(2,128)} %bitcast.698, f32[]{:T(128)} %constant.5.clone.1), dimensions={2,4,6}, to_apply=%region_0.1 | reduce | flops 458752 | bytes 2359300 | tf_op jit(solution)/shard_map/reduce_sum | solution.py:31
  76.7 4.8 collective-permute-start.2
  81.6 1.3 collective-permute-start.3
  84.5 8.7 %copy.335 = f32[4,64,8,9,32]{1,4,3,2,0:T(8,128)} copy(f32[4,64,8,9,32]{4,2,3,1,0:T(8,128)} %get-tuple-element.9) | data formatting | bytes 4718592 | tf_op jit(solution)/shard_map/jit(_where)/select_n | solution.py:25
  93.9 2.3 pad_maximum_fusion
  96.2 3.8 copy.455
  100.0 2.6 pad.12.clone
  102.6 3.0 copy.333
  105.6 1.2 slice.258
  106.8 4.6 compare_select_fusion.1
  127.9 1.5 fusion.39
  132.9 3.0 collective-permute-start.4
  136.0 1.5 collective-permute-start.5
  137.4 1.6 copy.334
  141.5 5.1 fusion.32
  147.5 7.6 %broadcast_in_dim.44 = f32[32,2,2,32,2,32,2]{0,6,5,4,3,2,1:T(2,128)} broadcast(f32[32,2,32,32]{0,3,2,1:T(8,128)S(1)} %copy.341), dimensions={0,1,3,5} | broadcast | bytes 2359296 | tf_op jit(solution)/shard_map/broadcast_in_dim | solution.py:36
  155.1 7.8 %copy.342 = f32[1,32,4,64,64]{3,1,4,2,0:T(8,128)} copy(f32[1,32,4,64,64]{1,4,3,2,0:T(8,128)} %bitcast.699) | data formatting | bytes 4194304 | tf_op jit(solution)/shard_map/broadcast_in_dim | solution.py:36
  163.0 5.8 fusion.14
  168.8 5.7 copy.343
  192.9 214.0 %all-reduce.5.cloned.1.call-done = f32[3,3,3,32,64]{4,3,2,1,0:T(8,128)} async-done(((f32[3,3,3,32,64]{4,3,2,1,0:T(8,128)}), f32[3,3,3,32,64]{4,3,2,1,0:T(8,128)}) %all-reduce.5.cloned.1.call-update) | async-done | bytes 221200 | tf_op jit(solution)/shard_map/psum | solution.py:92
  407.7 138.2 %psum.28 = f32[3,3,3,4,32]{4,3,2,1,0:T(4,128)S(1)} all-reduce(f32[3,3,3,4,32]{4,3,2,1,0:T(4,128)S(1)} %bitcast.714), channel_id=1, replica_groups=mesh['dp'=8,'space'=32] {'space'}, use_global_device_ids=true, to_apply=%region_3.4 | all-reduce | flops 3456 | bytes 27648 | tf_op jit(solution)/shard_map/psum | solution.py:92
  545.8 53.9 %psum.29 = f32[3,3,3,4,32]{4,3,2,1,0:T(4,128)} all-reduce(f32[3,3,3,4,32]{4,3,2,1,0:T(4,128)S(1)} %psum.28), channel_id=1, replica_groups=mesh['dp'=8,'space'=32] {'dp'}, use_global_device_ids=true, to_apply=%region_4.5 | all-reduce | flops 3456 | bytes 27648 | tf_op jit(solution)/shard_map/psum | solution.py:92
  599.8 1.8 copy.567
  (126 shorter events, 48.8 us)
Async XLA Ops:
  7.2 99.6 %copy-start = (bf16[3,3,3,32,64]{4,3,2,1,0:T(8,128)(2,1)S(1)}, bf16[3,3,3,32,64]{4,3,2,1,0:T(8,128)(2,1)}, u32[]{:S(2)}) copy-start(bf16[3,3,3,32,64]{4,3,2,1,0:T(8,128)(2,1)} %param.6) | copy-start | bytes 331780
  7.2 399.7 %all-reduce.5.cloned.1.call-start = ((), (), s32[]{:S(2)}) async-start(), calls=%async_computation | async-start | bytes 884736 | tf_op jit(solution)/shard_map/psum | solution.py:92
  8.5 2.6 collective-permute-start
  9.8 3.2 collective-permute-start.1
  11.1 0.6 copy-start.10
  13.0 0.6 copy-start.8
  14.1 5.4 copy-start.14
  14.1 5.4 copy-start.15
  75.8 7.0 %copy-start.13 = (bf16[1,64,1,16,16]{1,4,3,2,0:T(8,128)(2,1)S(1)}, bf16[1,64,1,16,16]{1,4,3,2,0:T(8,128)(2,1)}, u32[]{:S(2)}) copy-start(bf16[1,64,1,16,16]{1,4,3,2,0:T(8,128)(2,1)} %param.7) | copy-start | bytes 98308
  75.9 7.7 %copy-start.3 = (bf16[1,4,4,64,64]{4,3,2,1,0:T(8,128)(2,1)S(1)}, bf16[1,4,4,64,64]{4,3,2,1,0:T(8,128)(2,1)}, u32[]{:S(2)}) copy-start(bf16[1,4,4,64,64]{4,3,2,1,0:T(8,128)(2,1)} %param.4) | copy-start | bytes 393220
  76.7 16.4 %collective-permute-start.2 = (bf16[1,32,1,32,32]{4,1,3,2,0:T(8,128)(2,1)}, bf16[1,32,1,32,32]{4,1,3,2,0:T(8,128)(2,1)S(1)}, u32[]{:S(2)}, u32[]{:S(2)}) collective-permute-start(bf16[1,32,1,32,32]{4,1,3,2,0:T(8,128)(2,1)} %get-tuple-element.17), channel_id=1, source_target_pairs={{0,1},{1,2},{2,3},{3,4},{4,5},{5,6},{6,7},{7,8},{8,9},{9,10},{10,1... | collective-permute-start | bytes 196616 | tf_op jit(solution)/shard_map/ppermute | solution.py:14
  81.6 12.3 %collective-permute-start.3 = (bf16[1,32,1,32,32]{4,1,3,2,0:T(8,128)(2,1)S(1)}, bf16[1,32,1,32,32]{4,1,3,2,0:T(8,128)(2,1)}, u32[]{:S(2)}, u32[]{:S(2)}) collective-permute-start(bf16[1,32,1,32,32]{4,1,3,2,0:T(8,128)(2,1)S(1)} %get-tuple-element.18), channel_id=1, source_target_pairs={{1,0},{2,1},{3,2},{4,3},{5,4},{6,5},{7,6},{8,7},{9,8},{10,9},{11,1... | collective-permute-start | bytes 196616 | tf_op jit(solution)/shard_map/ppermute | solution.py:15
  93.2 0.7 copy-start.6
  102.6 4.2 copy-start.16
  111.4 0.9 copy-start.4
  114.4 1.9 copy-start.7
  130.8 2.1 copy-start.2
  132.0 0.8 copy-start.5
  132.8 467.0 %all-reduce.7.cloned.1.call-start = ((), (), s32[]{:S(2)}) async-start(), calls=%async_computation.1 | async-start | bytes 884736 | tf_op jit(solution)/shard_map/psum | solution.py:92
  132.9 7.3 %collective-permute-start.4 = (bf16[1,64,1,32,32]{1,3,4,2,0:T(8,128)(2,1)S(1)}, bf16[1,64,1,32,32]{1,3,4,2,0:T(8,128)(2,1)S(1)}, u32[]{:S(2)}, u32[]{:S(2)}) collective-permute-start(bf16[1,64,1,32,32]{1,3,4,2,0:T(8,128)(2,1)S(1)} %get-tuple-element.15), channel_id=1, source_target_pairs={{0,1},{1,2},{2,3},{3,4},{4,5},{5,6},{6,7},{7,8},{8,9},{9,10},{10,1... | collective-permute-start | bytes 393224 | tf_op jit(solution)/shard_map/ppermute | solution.py:14
  136.0 4.3 collective-permute-start.5
  175.9 1.5 copy-start.11
  182.2 1.6 copy-start.1
  182.2 1.6 copy-start.12
  188.7 1.5 copy-start.9
Sparse Core Ops, SparseCore 0:
  132.9 273.9 all-reduce.4
  409.8 107.0 all-reduce.6
